TPU v7x, 128 devices: a whole 4x4x4 slice. The times are simulated.
128 devices in a mesh: grp: 8 (over x, core), hub: 16 (over y, z).
Axes of the slice: x: 4, y: 4, z: 4, core: 2. Of those that a mesh axis runs over, the one named last changes fastest.
Arguments:
- embed: bfloat16 [1048576, 128], P(('grp', 'hub')), may hold values from -6 to 6
- hub_ids: int32 [128, 4], P(('grp', 'hub')), may hold values from 0 to 63
- send_ids: int32 [128, 8, 4], P(('grp', 'hub')), may hold values from 0 to 63
- tile_row: int32 [128, 192], P(('grp', 'hub')), may hold values from 0 to 63
- tile_col: int32 [128, 192], P(('grp', 'hub')), may hold values from 0 to 159
- tile_val: bfloat16 [24576, 128, 128], P(('grp', 'hub')), may hold values from -0.3125 to 0.3125
- tile_count: int32 [128], P(('grp', 'hub')), may hold values from 96 to 192, as said below
Outputs:
- spectral: float32 [1048576, 128], P(('grp', 'hub'))
Inputs may be any that keep to these rules, and one draw needn't show every extreme that they name: `tile_count`: each device has at least 96 live tile slots and some device has all 192 live; slots at or past a device's count are ignored.
All inputs are finite; a program needn't handle non-finite values.
Results may differ from a plain program's by a relative error of at most 0.0051.
Values may be sent and summed in bfloat16 or wider, within the bound.
A program may use at most 128 MiB of HBM per device.

v0:
```python
import math

import jax
import jax.numpy as jnp
from jax import lax
from jax.sharding import Mesh
from jax.sharding import PartitionSpec as P

ORDER = 4
HUB = ("hub_0", "hub_1")
GRP_HUB = ("grp", "hub_0", "hub_1")


SHIFT = 0.2
THETA = 3.0


def whole_of(shard, axes, dim):
    result = shard
    for number in range(len(axes) - 1, -1, -1):
        result = lax.all_gather(result, axes[number], axis=dim, tiled=True)
    return result


def bessel_scaled(order_index):
    total = 0.0
    for term in range(40):
        total += (THETA / 2.0) ** (2 * term + order_index) / (
            math.factorial(term) * math.factorial(term + order_index)
        )
    return math.exp(-THETA) * total


def coefficients():
    values = [bessel_scaled(0)]
    for order_index in range(1, ORDER + 1):
        values.append(2.0 * (-1.0) ** order_index * bessel_scaled(order_index))
    return values


def shards(embed, hub_ids, send_ids, tile_row, tile_col, tile_val, tile_count):
    width = embed.shape[1]
    tile_size = tile_val.shape[1]
    nblocks = embed.shape[0] // tile_size
    slots = tile_val.shape[0]
    live = (jnp.arange(slots, dtype=jnp.int32) < tile_count[0]).astype(jnp.float32)
    row_list = tile_row[0]
    hub_list = hub_ids[0]
    send_list = send_ids[0].reshape(-1)
    col_list = tile_col[0]

    def apply(field):
        blocks = field.reshape(nblocks, tile_size, width)
        hub_local = blocks[hub_list].reshape(-1, width)
        hub_all = whole_of(hub_local, HUB, 0)
        outgoing = blocks[send_list].reshape(-1, width)
        tail = lax.all_to_all(outgoing, "grp", split_axis=0, concat_axis=0, tiled=True)
        space = jnp.concatenate([field, hub_all, tail], axis=0).reshape(-1, tile_size, width)
        picked = space[col_list]
        prod = jnp.einsum("tij,tjk->tik", tile_val, picked, preferred_element_type=jnp.float32)
        masked = prod * live[:, None, None]
        summed = jax.ops.segment_sum(masked, row_list, num_segments=nblocks)
        return summed.reshape(nblocks * tile_size, width) - SHIFT * field.astype(jnp.float32)

    weights = coefficients()
    previous = embed
    spectral = weights[0] * previous.astype(jnp.float32)
    current = apply(previous).astype(jnp.bfloat16)
    spectral = spectral + weights[1] * current.astype(jnp.float32)
    for order_index in range(2, ORDER + 1):
        following = (2.0 * apply(current) - previous.astype(jnp.float32)).astype(jnp.bfloat16)
        spectral = spectral + weights[order_index] * following.astype(jnp.float32)
        previous, current = (current, following)
    return spectral


def solution(mesh):
    finer = Mesh(mesh.devices.reshape(mesh.shape["grp"], 4, 4), ("grp", "hub_0", "hub_1"))
    in_specs = (
        P(GRP_HUB, None),
        P(GRP_HUB, None),
        P(GRP_HUB, None, None),
        P(GRP_HUB, None),
        P(GRP_HUB, None),
        P(GRP_HUB, None, None),
        P(GRP_HUB),
    )
    out_specs = P(GRP_HUB, None)
    return jax.shard_map(
        shards, mesh=finer, in_specs=in_specs, out_specs=out_specs, check_vma=False
    )
```

profile of v0, /device:TPU:4, one launch (start us, length us, event | category | flops | bytes accessed | tf_op | source)
XLA Modules:
  0.0 616.3 jit_solution(8018080672462354423)
XLA Ops:
  7.4 2.2 gather_fusion
  9.5 14.7 %all_gather.24 = bf16[2048,128]{1,0:T(8,128)(2,1)} all-gather(bf16[512,128]{1,0:T(8,128)(2,1)S(1)} %bitcast.79), channel_id=1, replica_groups=mesh['grp'=8,'hub_0'=4,'hub_1'=4] {'hub_1'}, dimensions={0}, use_global_device_ids=true | all-gather | bytes 655360 | tf_op jit(solution)/shard_map/all_gather | solution.py:21
  25.1 3.2 gather_fusion.1
  28.4 4.8 all-to-all-start
  33.9 12.1 %all-to-all-done = bf16[8,512,128]{2,1,0:T(8,128)(2,1)S(1)} async-done(((bf16[8,512,128]{2,1,0:T(8,128)(2,1)}), bf16[8,512,128]{2,1,0:T(8,128)(2,1)S(1)}, u32[]{:S(2)}, u32[]{:S(2)}) %all-to-all-start) | async-done | bytes 1048608 | tf_op jit(solution)/shard_map/all_to_all | solution.py:57
  46.0 11.0 %all-gather.5.cloned.1.call-done = bf16[8192,128]{1,0:T(8,128)(2,1)} async-done(((bf16[2048,128]{1,0:T(8,128)(2,1)}), bf16[8192,128]{1,0:T(8,128)(2,1)}) %all-gather.5.cloned.1.call-update) | async-done | bytes 2097168 | tf_op jit(solution)/shard_map/all_gather | solution.py:21
  57.0 22.8 %pad_maximum_fusion = bf16[20480,128]{1,0:T(8,128)(2,1)} fusion(bf16[4096,128]{1,0:T(8,128)(2,1)S(1)} %bitcast.70, bf16[8192,128]{1,0:T(8,128)(2,1)} %all-gather.5.cloned.1.call-done, bf16[8192,128]{1,0:T(8,128)(2,1)S(1)} %copy-done), kind=kLoop, calls=%fused_computation.31 | loop fusion | flops 15728640 | bytes 10485760 | tf_op jit(solution)/shard_map/concatenate | solution.py:58
  79.9 10.7 %gather_fusion.2 = bf16[192,128,128]{2,1,0:T(8,128)(2,1)} fusion(bf16[160,128,128]{2,1,0:T(8,128)(2,1)} %bitcast.67, s32[1024]{0:T(1024)S(1)} %pad_clamp_fusion), kind=kCustom, calls=%fused_computation.2 | custom fusion | bytes 12583680 | tf_op jit(solution)/shard_map/gather | solution.py:59
  90.5 13.8 %multiply_bitcast_fusion.3 = f32[192,128,128]{1,2,0:T(8,128)} fusion(f32[192]{0:T(256)S(1)} %compare_convert_fusion, bf16[192,128,128]{2,1,0:T(8,128)(2,1)} %gather_fusion.2, bf16[192,128,128]{2,1,0:T(8,128)(2,1)} %param.12), kind=kOutput, calls=%fused_computation.19 | convolution fusion | flops 808452096 | bytes 25166592 | tf_op jit(solution)/shard_map/tij,tjk->tik/dot_general | solution.py:60
  104.3 12.6 %copy.15 = f32[192,128,128]{2,1,0:T(8,128)} copy(f32[192,128,128]{1,2,0:T(8,128)} %multiply_bitcast_fusion.3) | data formatting | bytes 25165824 | tf_op jit(solution)/shard_map/mul | solution.py:61
  116.9 2.5 broadcast.77.clone
  119.4 39.0 %scatter_fusion = f32[64,128,128]{2,1,0:T(8,128)} fusion(f32[64,128,128]{2,1,0:T(8,128)} %broadcast.77.clone, s32[192]{0:T(256)S(1)} %bitcast.82, f32[192,128,128]{2,1,0:T(8,128)} %copy.15), kind=kCustom, calls=%fused_computation.12 | custom fusion | flops 3145728 | bytes 37749504 | tf_op jit(solution)/shard_map/scatter-add | solution.py:62
  158.4 3.4 fusion.7
  162.4 13.9 %all_gather.26 = bf16[2048,128]{1,0:T(8,128)(2,1)} all-gather(bf16[512,128]{1,0:T(8,128)(2,1)S(1)} %bitcast.80), channel_id=1, replica_groups=mesh['grp'=8,'hub_0'=4,'hub_1'=4] {'hub_1'}, dimensions={0}, use_global_device_ids=true | all-gather | bytes 655360 | tf_op jit(solution)/shard_map/all_gather | solution.py:21
  176.3 1.7 gather_fusion.4
  178.0 17.7 %all_to_all.48 = bf16[8,512,128]{2,1,0:T(8,128)(2,1)S(1)} all-to-all(bf16[8,512,128]{2,1,0:T(8,128)(2,1)} %bitcast.76), channel_id=1, replica_groups=mesh['grp'=8,'hub_0'=4,'hub_1'=4] {'grp'}, dimensions={0} | all-to-all | bytes 2097152 | tf_op jit(solution)/shard_map/all_to_all | solution.py:57
  195.7 11.6 %all-gather.7.cloned.1.call-done = bf16[8192,128]{1,0:T(8,128)(2,1)} async-done(((bf16[2048,128]{1,0:T(8,128)(2,1)}), bf16[8192,128]{1,0:T(8,128)(2,1)}) %all-gather.7.cloned.1.call-update) | async-done | bytes 2097168 | tf_op jit(solution)/shard_map/all_gather | solution.py:21
  207.3 22.8 %pad_maximum_fusion.1 = bf16[20480,128]{1,0:T(8,128)(2,1)} fusion(bf16[4096,128]{1,0:T(8,128)(2,1)S(1)} %bitcast.71, bf16[8192,128]{1,0:T(8,128)(2,1)} %all-gather.7.cloned.1.call-done, bf16[8192,128]{1,0:T(8,128)(2,1)S(1)} %fusion.7), kind=kLoop, calls=%fused_computation.32 | loop fusion | flops 15728640 | bytes 10485760 | tf_op jit(solution)/shard_map/concatenate | solution.py:58
  230.2 10.9 %gather_fusion.5 = bf16[192,128,128]{2,1,0:T(8,128)(2,1)} fusion(bf16[160,128,128]{2,1,0:T(8,128)(2,1)} %bitcast.68, s32[1024]{0:T(1024)S(1)} %pad_clamp_fusion), kind=kCustom, calls=%fused_computation.5 | custom fusion | bytes 12583680 | tf_op jit(solution)/shard_map/gather | solution.py:59
  241.1 13.8 %multiply_bitcast_fusion.2 = f32[192,128,128]{1,2,0:T(8,128)} fusion(f32[192]{0:T(256)S(1)} %compare_convert_fusion, bf16[192,128,128]{2,1,0:T(8,128)(2,1)} %gather_fusion.5, bf16[192,128,128]{2,1,0:T(8,128)(2,1)} %param.12), kind=kOutput, calls=%fused_computation.18 | convolution fusion | flops 808452096 | bytes 25166592 | tf_op jit(solution)/shard_map/tij,tjk->tik/dot_general | solution.py:60
  254.8 12.6 %copy.17 = f32[192,128,128]{2,1,0:T(8,128)} copy(f32[192,128,128]{1,2,0:T(8,128)} %multiply_bitcast_fusion.2) | data formatting | bytes 25165824 | tf_op jit(solution)/shard_map/mul | solution.py:61
  267.4 2.5 broadcast.77.clone.1
  270.0 39.0 %scatter_fusion.1 = f32[64,128,128]{2,1,0:T(8,128)} fusion(f32[64,128,128]{2,1,0:T(8,128)} %broadcast.77.clone.1, s32[192]{0:T(256)S(1)} %bitcast.83, f32[192,128,128]{2,1,0:T(8,128)} %copy.17), kind=kCustom, calls=%fused_computation.13 | custom fusion | flops 3145728 | bytes 37749504 | tf_op jit(solution)/shard_map/scatter-add | solution.py:62
  308.9 5.1 fusion.8
  314.1 2.2 gather_fusion.6
  316.2 13.9 %all_gather.28 = bf16[2048,128]{1,0:T(8,128)(2,1)} all-gather(bf16[512,128]{1,0:T(8,128)(2,1)S(1)} %bitcast.81), channel_id=1, replica_groups=mesh['grp'=8,'hub_0'=4,'hub_1'=4] {'hub_1'}, dimensions={0}, use_global_device_ids=true | all-gather | bytes 655360 | tf_op jit(solution)/shard_map/all_gather | solution.py:21
  330.2 3.2 gather_fusion.7
  333.4 17.9 %all_to_all.49 = bf16[8,512,128]{2,1,0:T(8,128)(2,1)S(1)} all-to-all(bf16[8,512,128]{2,1,0:T(8,128)(2,1)} %bitcast.77), channel_id=1, replica_groups=mesh['grp'=8,'hub_0'=4,'hub_1'=4] {'grp'}, dimensions={0} | all-to-all | bytes 2097152 | tf_op jit(solution)/shard_map/all_to_all | solution.py:57
  351.3 9.9 %all-gather.9.cloned.1.call-done = bf16[8192,128]{1,0:T(8,128)(2,1)} async-done(((bf16[2048,128]{1,0:T(8,128)(2,1)}), bf16[8192,128]{1,0:T(8,128)(2,1)}) %all-gather.9.cloned.1.call-update) | async-done | bytes 2097168 | tf_op jit(solution)/shard_map/all_gather | solution.py:21
  361.2 16.2 %pad_maximum_fusion.2 = bf16[20480,128]{1,0:T(8,128)(2,1)} fusion(bf16[4096,128]{1,0:T(8,128)(2,1)S(1)} %bitcast.72, bf16[8192,128]{1,0:T(8,128)(2,1)} %all-gather.9.cloned.1.call-done, bf16[8192,128]{1,0:T(8,128)(2,1)} %fusion.8), kind=kLoop, calls=%fused_computation.33 | loop fusion | flops 15728640 | bytes 10485760 | tf_op jit(solution)/shard_map/concatenate | solution.py:58
  377.4 10.5 %gather_fusion.8 = bf16[192,128,128]{2,1,0:T(8,128)(2,1)} fusion(bf16[160,128,128]{2,1,0:T(8,128)(2,1)} %bitcast.69, s32[1024]{0:T(1024)S(1)} %pad_clamp_fusion), kind=kCustom, calls=%fused_computation.8 | custom fusion | bytes 12583680 | tf_op jit(solution)/shard_map/gather | solution.py:59
  387.9 13.8 %multiply_bitcast_fusion.1 = f32[192,128,128]{1,2,0:T(8,128)} fusion(f32[192]{0:T(256)S(1)} %compare_convert_fusion, bf16[192,128,128]{2,1,0:T(8,128)(2,1)} %gather_fusion.8, bf16[192,128,128]{2,1,0:T(8,128)(2,1)} %param.12), kind=kOutput, calls=%fused_computation.17 | convolution fusion | flops 808452096 | bytes 25166592 | tf_op jit(solution)/shard_map/tij,tjk->tik/dot_general | solution.py:60
  401.6 12.6 %copy.19 = f32[192,128,128]{2,1,0:T(8,128)} copy(f32[192,128,128]{1,2,0:T(8,128)} %multiply_bitcast_fusion.1) | data formatting | bytes 25165824 | tf_op jit(solution)/shard_map/mul | solution.py:61
  414.2 2.5 broadcast.77.clone.2
  416.8 39.0 %scatter_fusion.2 = f32[64,128,128]{2,1,0:T(8,128)} fusion(f32[64,128,128]{2,1,0:T(8,128)} %broadcast.77.clone.2, s32[192]{0:T(256)S(1)} %bitcast.84, f32[192,128,128]{2,1,0:T(8,128)} %copy.19), kind=kCustom, calls=%fused_computation.14 | custom fusion | flops 3145728 | bytes 37749504 | tf_op jit(solution)/shard_map/scatter-add | solution.py:62
  455.7 5.1 fusion.11
  460.8 2.2 gather_fusion.9
  463.0 13.9 %all_gather.30 = bf16[2048,128]{1,0:T(8,128)(2,1)} all-gather(bf16[512,128]{1,0:T(8,128)(2,1)S(1)} %bitcast.78), channel_id=1, replica_groups=mesh['grp'=8,'hub_0'=4,'hub_1'=4] {'hub_1'}, dimensions={0}, use_global_device_ids=true | all-gather | bytes 655360 | tf_op jit(solution)/shard_map/all_gather | solution.py:21
  476.9 3.2 gather_fusion.10
  480.2 17.9 %all_to_all.50 = bf16[8,512,128]{2,1,0:T(8,128)(2,1)S(1)} all-to-all(bf16[8,512,128]{2,1,0:T(8,128)(2,1)} %bitcast.75), channel_id=1, replica_groups=mesh['grp'=8,'hub_0'=4,'hub_1'=4] {'grp'}, dimensions={0} | all-to-all | bytes 2097152 | tf_op jit(solution)/shard_map/all_to_all | solution.py:57
  498.1 9.9 %all-gather.11.cloned.1.call-done = bf16[8192,128]{1,0:T(8,128)(2,1)} async-done(((bf16[2048,128]{1,0:T(8,128)(2,1)}), bf16[8192,128]{1,0:T(8,128)(2,1)}) %all-gather.11.cloned.1.call-update) | async-done | bytes 2097168 | tf_op jit(solution)/shard_map/all_gather | solution.py:21
  508.0 16.2 %pad_maximum_fusion.3 = bf16[20480,128]{1,0:T(8,128)(2,1)} fusion(bf16[4096,128]{1,0:T(8,128)(2,1)S(1)} %bitcast.73, bf16[8192,128]{1,0:T(8,128)(2,1)} %all-gather.11.cloned.1.call-done, bf16[8192,128]{1,0:T(8,128)(2,1)} %fusion.11), kind=kLoop, calls=%fused_computation.34 | loop fusion | flops 15728640 | bytes 10485760 | tf_op jit(solution)/shard_map/concatenate | solution.py:58
  524.2 10.5 %gather_fusion.11 = bf16[192,128,128]{2,1,0:T(8,128)(2,1)} fusion(bf16[160,128,128]{2,1,0:T(8,128)(2,1)} %bitcast.66, s32[1024]{0:T(1024)S(1)} %pad_clamp_fusion), kind=kCustom, calls=%fused_computation.11 | custom fusion | bytes 12583680 | tf_op jit(solution)/shard_map/gather | solution.py:59
  534.7 13.7 %multiply_bitcast_fusion = f32[192,128,128]{1,2,0:T(8,128)} fusion(f32[192]{0:T(256)S(1)} %compare_convert_fusion, bf16[192,128,128]{2,1,0:T(8,128)(2,1)} %gather_fusion.11, bf16[192,128,128]{2,1,0:T(8,128)(2,1)} %param.12), kind=kOutput, calls=%fused_computation.16 | convolution fusion | flops 808452096 | bytes 25166592 | tf_op jit(solution)/shard_map/tij,tjk->tik/dot_general | solution.py:60
  548.4 12.6 %copy.21 = f32[192,128,128]{2,1,0:T(8,128)} copy(f32[192,128,128]{1,2,0:T(8,128)} %multiply_bitcast_fusion) | data formatting | bytes 25165824 | tf_op jit(solution)/shard_map/mul | solution.py:61
  560.9 2.5 broadcast.77
  563.4 39.4 %scatter_fusion.3 = f32[64,128,128]{2,1,0:T(8,128)} fusion(f32[64,128,128]{2,1,0:T(8,128)} %broadcast.77, s32[192]{0:T(256)S(1)} %bitcast.85, f32[192,128,128]{2,1,0:T(8,128)} %copy.21), kind=kCustom, calls=%fused_computation.15 | custom fusion | flops 3145728 | bytes 37749504 | tf_op jit(solution)/shard_map/scatter-add | solution.py:62
  602.8 6.6 %fusion.1 = f32[8192,128]{1,0:T(8,128)} fusion(bf16[8192,128]{1,0:T(8,128)(2,1)} %fusion.11, bf16[8192,128]{1,0:T(8,128)(2,1)} %param.7, bf16[8192,128]{1,0:T(8,128)(2,1)S(1)} %fusion.7, bf16[8192,128]{1,0:T(8,128)(2,1)} %fusion.8, f32[64,128,128]{2,1,0:T(8,128)} %scatter_fusion.3), kind=kLoop, calls=%fused_computation.36 | loop fusion | flops 19922944 | bytes 16777216 | tf_op jit(solution)/shard_map/add | solution.py:72
  (24 shorter events, 2.4 us)
Async XLA Ops:
  6.5 50.5 %copy-start = (bf16[8192,128]{1,0:T(8,128)(2,1)S(1)}, bf16[8192,128]{1,0:T(8,128)(2,1)}, u32[]{:S(2)}) copy-start(bf16[8192,128]{1,0:T(8,128)(2,1)} %param.7) | copy-start | bytes 6291460
  6.5 27.3 %copy-start.2 = (s32[1,192]{1,0:T(1,128)S(1)}, s32[1,192]{1,0:T(1,128)}, u32[]{:S(2)}) copy-start(s32[1,192]{1,0:T(1,128)} %param.11) | copy-start | bytes 2308
  6.5 50.5 %all-gather.5.cloned.1.call-start = ((), (), s32[]{:S(2)}) async-start(), calls=%async_computation.4 | async-start | bytes 2621440 | tf_op jit(solution)/shard_map/all_gather | solution.py:21
  28.4 17.6 %all-to-all-start = ((bf16[8,512,128]{2,1,0:T(8,128)(2,1)}), bf16[8,512,128]{2,1,0:T(8,128)(2,1)S(1)}, u32[]{:S(2)}, u32[]{:S(2)}) async-start(bf16[8,512,128]{2,1,0:T(8,128)(2,1)} %bitcast.74), calls=%async_computation | async-start | bytes 2097152 | tf_op jit(solution)/shard_map/all_to_all | solution.py:57
  33.2 174.1 %all-gather.7.cloned.1.call-start = ((), (), s32[]{:S(2)}) async-start(), calls=%async_computation.5 | async-start | bytes 2621440 | tf_op jit(solution)/shard_map/all_gather | solution.py:21
  104.3 15.1 %copy-start.1 = (s32[1,192]{1,0:T(1,128)S(1)}, s32[1,192]{1,0:T(1,128)}, u32[]{:S(2)}) copy-start(s32[1,192]{1,0:T(1,128)} %param.10) | copy-start | bytes 2308
  176.3 184.9 %all-gather.9.cloned.1.call-start = ((), (), s32[]{:S(2)}) async-start(), calls=%async_computation.6 | async-start | bytes 2621440 | tf_op jit(solution)/shard_map/all_gather | solution.py:21
  330.1 177.8 %all-gather.11.cloned.1.call-start = ((), (), s32[]{:S(2)}) async-start(), calls=%async_computation.7 | async-start | bytes 2621440 | tf_op jit(solution)/shard_map/all_gather | solution.py:21
Sparse Core Ops, SparseCore 0:
  24.4 32.5 all-gather.4
  176.4 30.8 all-gather.6
  330.3 30.8 all-gather.8
  477.0 30.8 all-gather.10
where the time goes:
time: 628 us; the launch traced here: 616 us
  other arithmetic  255 us (41%)
  local copies, waits for them, and re-layouts  122 us (19%)
  blocking collectives  110 us (18%)
  matrix products  54.9 us (9%)
  waiting for transfers between devices  54.6 us (9%)
  between operations  14.3 us (2%)
    scatter-add x4, other arithmetic, apply(): summed = jax.ops.segment_sum(masked, row_list, num_segments=nblocks)  156 us
    concatenate x4, other arithmetic, apply(): jnp.concatenate([field, hub_all, tail], axis=0)  78.1 us
    all_gather x4, blocking collectives, whole_of(): result = lax.all_gather(result, axes[number], axis=dim, tiled=True)  56.4 us
    dot_general x4, matrix products, apply(): jnp.einsum('tij,tjk->tik', tile_val, picked, preferred_element_type=jnp.f...  54.9 us
    all_to_all x3, blocking collectives, apply(): lax.all_to_all(outgoing, 'grp', split_axis=0, concat_axis=0, tiled=True)  53.6 us
    mul x4, local copies, waits for them, and re-layouts, apply(): masked = prod * live[:, None, None]  50.4 us
    gather x4, local copies, waits for them, and re-layouts, apply(): picked = space[col_list]  42.5 us
    all_gather x4, waiting for transfers between devices, whole_of(): result = lax.all_gather(result, axes[number], axis=dim, tiled=True)  42.4 us
  transfers between devices with their start and end apart: 5, of which 5 were waited for; matrix products, arithmetic and copies ran while one was open for 2% of the time, Pallas kernels for 0%

commit v1 on v0

v1 whole, which is shorter than its diff:
```python
import functools
import math

import jax
import jax.numpy as jnp
from jax import lax
from jax.experimental import pallas as pl
from jax.experimental.pallas import tpu as pltpu
from jax.sharding import PartitionSpec as P

ORDER = 4
SHIFT = 0.2
THETA = 3.0
MESH = pl.DeviceIdType.MESH

NB = 64
TILES = 192
HUB0 = 64
TAIL0 = 128
COLS = 160
BLK = 128
EMB = 128
UNROLL = 8

TAILS = ((2, 0), (2, 1), (1, 0), (1, 1), (3, 0), (3, 1), (0, 1))
NAMES = ("m1p", "m1m", "m2p", "m2m")
for _q in (0, -1, 1):
    NAMES += tuple(f"{s}{_q}" for s in ("s1p", "s1m", "s2p", "s2m"))
NAMES += ("s1p2a", "s1p2b", "s1m2a", "s1m2b", "s2p2", "s2m2")
NHUB = len(NAMES)
NMSG = 2 * NHUB + len(TAILS)


def bessel_scaled(order_index):
    total = 0.0
    for term in range(40):
        total += (THETA / 2.0) ** (2 * term + order_index) / (
            math.factorial(term) * math.factorial(term + order_index)
        )
    return math.exp(-THETA) * total


def coefficients():
    values = [bessel_scaled(0)]
    for order_index in range(1, ORDER + 1):
        values.append(2.0 * (-1.0) ** order_index * bessel_scaled(order_index))
    return values


def kernel(
    cols, prev, last, hub_ids, send_ids, embed, tile_val, out,
    sp0, sp1, sp2, sp3, start, tiles, sums, outgoing, load_sem, tile_sem, send_sem, recv_sem,
):
    spaces = (sp0, sp1, sp2, sp3)
    coef = coefficients()
    grp = lax.axis_index("grp")
    hub = lax.axis_index("hub")
    x, core = grp // 2, grp % 2
    y, z = hub // 4, hub % 4

    load0 = pltpu.make_async_copy(embed, start, load_sem.at[0])
    load0.start()
    load1 = pltpu.make_async_copy(embed, sp0.at[pl.ds(0, NB)], load_sem.at[1])
    load1.start()
    quarter = TILES // 4
    loads = []
    for part in range(4):
        cut = pl.ds(part * quarter, quarter)
        loads.append(pltpu.make_async_copy(tile_val.at[cut], tiles.at[cut], tile_sem.at[part]))
        loads[-1].start()

    def place(fam, d1, d2):
        dy, dz = (d2, d1) if fam == 0 else (d1, d2)
        return ((y + dy + 4) % 4) * 4 + (z + dz + 4) % 4

    def tail_group(dx, dc):
        return ((x + dx) % 4) * 2 + (core + dc) % 2

    barrier = pltpu.get_barrier_semaphore()
    friends = [(grp, place(0, d1, d2)) for d1, d2 in ((1, 0), (-1, 0), (0, 1), (0, -1))]
    friends += [(tail_group(dx, dc), hub) for dx, dc in TAILS]
    for friend in friends:
        pl.semaphore_signal(barrier, inc=1, device_id=friend, device_id_type=MESH)

    plan = {
        "m1p": ((0, 0), 0, 2, (1, 0)),
        "m1m": ((0, 0), 0, 2, (-1, 0)),
        "m2p": ((-1, 0), 0, 1, (1, 0)),
        "m2m": ((1, 0), 1, 1, (-1, 0)),
    }
    for q in (0, -1, 1):
        plan[f"s1p{q}"] = ((q, 0), 0, 2, (0, 1))
        plan[f"s1m{q}"] = ((q, 0), 0, 2, (0, -1))
    plan["s1p2a"] = ((2, 0), 0, 1, (0, 1))
    plan["s1p2b"] = ((2, 0), 1, 1, (0, 1))
    plan["s1m2a"] = ((2, 0), 0, 1, (0, -1))
    plan["s1m2b"] = ((2, 0), 1, 1, (0, -1))
    for q in (0, -1, 1, 2):
        plan[f"s2p{q}"] = ((q, -1), 0, 1, (0, 1))
        plan[f"s2m{q}"] = ((q, 1), 1, 1, (0, -1))

    def hub_copy(step, fam, name, arriving=False):
        (r1, r2), first, count, (t1, t2) = plan[name]
        if arriving:
            r1, r2 = r1 - t1, r2 - t2
        r1, r2 = (r1 + 8) % 4, (r2 + 8) % 4
        region = pl.ds(HUB0 + place(fam, r1, r2) * 4 + fam * 2 + first, count)
        ident = fam * NHUB + NAMES.index(name)
        return pltpu.make_async_remote_copy(
            src_ref=spaces[step].at[region],
            dst_ref=spaces[step].at[region],
            send_sem=send_sem.at[step, ident],
            recv_sem=recv_sem.at[step, ident],
            device_id=(grp, place(fam, t1, t2)),
            device_id_type=MESH,
        )

    def tail_copy(step, number, arriving=False):
        dx, dc = TAILS[number]
        target = tail_group(dx, dc)
        source = tail_group(4 - dx, dc) if arriving else grp
        ident = 2 * NHUB + number
        return pltpu.make_async_remote_copy(
            src_ref=outgoing.at[pl.ds(target * 4, 4)],
            dst_ref=spaces[step].at[pl.ds(TAIL0 + source * 4, 4)],
            send_sem=send_sem.at[step, ident],
            recv_sem=recv_sem.at[step, ident],
            device_id=(target, hub),
            device_id_type=MESH,
        )

    def row_of(step, row):
        if step == 0:
            return start[row]
        value = sums[last[row]] - SHIFT * spaces[step - 1][row].astype(jnp.float32)
        if step >= 2:
            value = 2.0 * value - spaces[step - 2][row].astype(jnp.float32)
        return value.astype(jnp.bfloat16)

    sums[TILES] = jnp.zeros((BLK, EMB), jnp.float32)
    load0.wait()
    pl.semaphore_wait(barrier, len(friends))

    for step in range(ORDER):
        space = spaces[step]

        def go(name):
            for fam in (0, 1):
                hub_copy(step, fam, name).start()

        def pass_on(name, *then):
            for fam in (0, 1):
                hub_copy(step, fam, name, arriving=True).wait_recv()
                for other in then:
                    hub_copy(step, fam, other).start()

        for slot in range(4):
            space[HUB0 + hub * 4 + slot] = row_of(step, hub_ids[slot])
        for name in ("m1p", "m1m", "s1p0", "s1m0"):
            go(name)
        for number, (dx, dc) in enumerate(TAILS):
            target = tail_group(dx, dc)

            def export(slot, carry):
                outgoing[target * 4 + slot] = row_of(step, send_ids[target * 4 + slot])
                return carry

            lax.fori_loop(0, 4, export, 0)
            tail_copy(step, number).start()

        def keep_tail(slot, carry):
            space[TAIL0 + grp * 4 + slot] = row_of(step, send_ids[grp * 4 + slot])
            return carry

        lax.fori_loop(0, 4, keep_tail, 0)

        def own(row, carry):
            if step == 0:
                value = start[row]
                out[row] = coef[0] * value.astype(jnp.float32)
            else:
                value = row_of(step, row)
                space[row] = value
                out[row] = out[row] + coef[step] * value.astype(jnp.float32)
            return carry

        lax.fori_loop(0, NB, own, 0)

        pass_on("m1p", "m2p")
        pass_on("m1m", "m2m")
        for name in ("s1p-1", "s1m-1", "s1p1", "s1m1"):
            go(name)
        pass_on("s1p0", "s2p0")
        pass_on("s1m0", "s2m0")
        pass_on("m2p", "s1p2a", "s1m2a")
        pass_on("m2m", "s1p2b", "s1m2b")
        pass_on("s1p-1", "s2p-1")
        pass_on("s1m-1", "s2m-1")
        pass_on("s1p1", "s2p1")
        pass_on("s1m1", "s2m1")
        pass_on("s1p2a", "s2p2")
        pass_on("s1m2b", "s2m2")
        for name in ("s1p2b", "s1m2a", "s2p0", "s2m0", "s2p-1", "s2m-1", "s2p1", "s2m1", "s2p2", "s2m2"):
            pass_on(name)
        for number in range(len(TAILS)):
            tail_copy(step, number, arriving=True).wait_recv()
        for number in range(len(TAILS)):
            tail_copy(step, number).wait_send()
        for fam in (0, 1):
            for name in NAMES:
                hub_copy(step, fam, name).wait_send()
        if step == 0:
            load1.wait()
            for load in loads:
                load.wait()

        def multiply(group, carry):
            for inner in range(UNROLL):
                slot = group * UNROLL + inner
                product = jnp.dot(tiles[slot], space[cols[slot]], preferred_element_type=jnp.float32)
                sums[slot] = sums[prev[slot]] + product
            return carry

        lax.fori_loop(0, TILES // UNROLL, multiply, 0)

    def finish(row, carry):
        value = row_of(ORDER, row)
        out[row] = out[row] + coef[ORDER] * value.astype(jnp.float32)
        return carry

    lax.fori_loop(0, NB, finish, 0)


def shards(embed, hub_ids, send_ids, tile_row, tile_col, tile_val, tile_count):
    slots = jnp.arange(TILES, dtype=jnp.int32)
    rows = tile_row[0]
    key = jnp.where(slots < tile_count[0], rows, -1)
    seen = jnp.where((key[None, :] == rows[:, None]) & (slots[None, :] < slots[:, None]), slots[None, :], -1)
    prev = jnp.max(seen, axis=1)
    prev = jnp.where(prev < 0, TILES, prev)
    blocks = jnp.arange(NB, dtype=jnp.int32)
    last = jnp.max(jnp.where(key[None, :] == blocks[:, None], slots[None, :], -1), axis=1)
    last = jnp.where(last < 0, TILES, last)

    smem = pl.BlockSpec(memory_space=pltpu.SMEM)
    hbm = pl.BlockSpec(memory_space=pl.ANY)
    out = pl.pallas_call(
        kernel,
        out_shape=jax.ShapeDtypeStruct((NB, BLK, EMB), jnp.float32),
        in_specs=[smem] * 5 + [hbm] * 2,
        out_specs=pl.BlockSpec(memory_space=pltpu.VMEM),
        scratch_shapes=[pltpu.VMEM((COLS, BLK, EMB), jnp.bfloat16)] * 4
        + [
            pltpu.VMEM((NB, BLK, EMB), jnp.bfloat16),
            pltpu.VMEM((TILES, BLK, BLK), jnp.bfloat16),
            pltpu.VMEM((TILES + 1, BLK, EMB), jnp.float32),
            pltpu.VMEM((32, BLK, EMB), jnp.bfloat16),
            pltpu.SemaphoreType.DMA((2,)),
            pltpu.SemaphoreType.DMA((4,)),
            pltpu.SemaphoreType.DMA((ORDER, NMSG)),
            pltpu.SemaphoreType.DMA((ORDER, NMSG)),
        ],
        compiler_params=pltpu.CompilerParams(
            collective_id=0, has_side_effects=True, vmem_limit_bytes=60 * 1024 * 1024
        ),
    )(
        tile_col[0], prev, last, hub_ids[0], send_ids[0].reshape(-1),
        embed.reshape(NB, BLK, EMB), tile_val,
    )
    return out.reshape(NB * BLK, EMB)


def solution(mesh):
    both = ("grp", "hub")
    return jax.shard_map(
        shards,
        mesh=mesh,
        in_specs=(
            P(both, None), P(both, None), P(both, None, None), P(both, None),
            P(both, None), P(both, None, None), P(both),
        ),
        out_specs=P(both, None),
        check_vma=False,
    )
```

time: 628 us -> 107 us (0.17); the launches traced: 616 us -> 106 us
  other arithmetic: 255 us -> 2.76 us
  local copies, waits for them, and re-layouts: 122 us -> 5.85 us
  blocking collectives: 110 us -> 0 us
  Pallas kernels: 0 us -> 96.4 us
  matrix products: 54.9 us -> 0 us
  waiting for transfers between devices: 54.6 us -> 0 us
  between operations: 14.3 us -> 0.67 us
    scatter-add x4 -> x0, other arithmetic: 156 us -> none  [apply(): summed = jax.ops.segment_sum(masked, row_list, num_segments=nblocks)]
    pallas_call x0 -> x1, Pallas kernels: none -> 96.4 us  [shards(): pl.pallas_call(kernel, out_shape=jax.ShapeDtypeStruct((NB, BLK, EMB), jnp...]
    concatenate x4 -> x0, other arithmetic: 78.1 us -> none  [apply(): jnp.concatenate([field, hub_all, tail], axis=0)]
    gather x12 -> x0, local copies, waits for them, and re-layouts: 61 us -> none  [the longest x4 42.5 us: apply(): picked = space[col_list]]
    all_gather x4 -> x0, blocking collectives: 56.4 us -> none  [whole_of(): result = lax.all_gather(result, axes[number], axis=dim, tiled=True)]
    dot_general x4 -> x0, matrix products: 54.9 us -> none  [apply(): jnp.einsum('tij,tjk->tik', tile_val, picked, preferred_element_type=jnp.f...]
    all_to_all x3 -> x0, blocking collectives: 53.6 us -> none  [apply(): lax.all_to_all(outgoing, 'grp', split_axis=0, concat_axis=0, tiled=True)]
    mul x4 -> x0, local copies, waits for them, and re-layouts: 50.4 us -> none  [apply(): masked = prod * live[:, None, None]]
  transfers between devices with their start and end apart: 5 -> 0, of which waited for: 5 -> 0; matrix products, arithmetic and copies ran while one was open for 2% -> 0% of each run, Pallas kernels for 0% -> 0%
where the time goes in v1:
time: 107 us; the launch traced here: 106 us
  Pallas kernels  96.4 us (90%)
  local copies, waits for them, and re-layouts  5.85 us (5%)
  other arithmetic  2.76 us (3%)
    pallas_call x1, Pallas kernels, shards(): pl.pallas_call(kernel, out_shape=jax.ShapeDtypeStruct((NB, BLK, EMB), jnp...  96.4 us
    unnamed x2, local copies, waits for them, and re-layouts  5.23 us

profile of v1, /device:TPU:4, one launch (start us, length us, event | category | flops | bytes accessed | tf_op | source)
XLA Modules:
  0.0 105.6 jit_solution(7099371097478021812)
XLA Ops:
  0.7 0.7 compare_select_fusion.1
  1.3 0.1 select_reduce_fusion.1
  1.5 0.9 select_reduce_fusion
  2.3 0.6 compare_select_fusion.prev
  2.9 0.5 compare_select_fusion.2.last
  3.4 0.8 copy.10
  4.2 0.6 reshape_squeeze.3.send_ids
  4.8 96.4 %shard_map.73 = f32[64,128,128]{2,1,0:T(8,128)} custom-call(s32[192]{0:T(256)} %bitcast.13, s32[192]{0:T(256)} %compare_select_fusion.prev, s32[64]{0:T(128)} %compare_select_fusion.2.last, s32[4]{0:T(128)} %bitcast.14, s32[32]{0:T(128)} %reshape_squeeze.3.send_ids, bf16[64,128,128]{2,1,0:T(8,128)(2,1)} %bitcast.9, bf16[192,128,128]{2,1,0:T(8,128)(2,1)} %tile_val.1), custom_call_target="tpu_custom_call" | custom-call | tf_op jit(solution)/shard_map/pallas_call | solution.py:247
  101.2 4.5 %copy.13 = f32[8192,128]{1,0:T(8,128)} copy(f32[8192,128]{1,0:T(8,128)} %bitcast.8) | data formatting | bytes 8388608

commit v2 on v1

v2 whole, which is shorter than its diff:
```python
import functools
import math

import jax
import jax.numpy as jnp
from jax import lax
from jax.experimental import pallas as pl
from jax.experimental.pallas import tpu as pltpu
from jax.sharding import PartitionSpec as P

ORDER = 4
SHIFT = 0.2
THETA = 3.0
MESH = pl.DeviceIdType.MESH

NB = 64
TILES = 192
HUB0 = 64
TAIL0 = 128
COLS = 160
BLK = 128
EMB = 128
UNROLL = 48

TAILS = ((2, 0), (2, 1), (1, 0), (1, 1), (3, 0), (3, 1), (0, 1))
PLAN = {
    "m1p": ((0, 0), 0, 2, (1, 0)),
    "m1m": ((0, 0), 0, 2, (-1, 0)),
    "m1d": ((0, 0), 0, 2, (2, 0)),
}
for _q in (0, -1, 1):
    PLAN[f"s1p{_q}"] = ((_q, 0), 0, 2, (0, 1))
    PLAN[f"s1m{_q}"] = ((_q, 0), 0, 2, (0, -1))
    PLAN[f"s2p{_q}"] = ((_q, -1), 0, 1, (0, 1))
    PLAN[f"s2m{_q}"] = ((_q, 1), 1, 1, (0, -1))
PLAN["s1p2"] = ((2, 0), 0, 2, (0, 1))
PLAN["s1m2"] = ((2, 0), 0, 2, (0, -1))
PLAN["s1d2"] = ((2, 0), 0, 2, (0, 2))
NAMES = tuple(PLAN)
NHUB = len(NAMES)
NMSG = 2 * NHUB + len(TAILS)


def bessel_scaled(order_index):
    total = 0.0
    for term in range(40):
        total += (THETA / 2.0) ** (2 * term + order_index) / (
            math.factorial(term) * math.factorial(term + order_index)
        )
    return math.exp(-THETA) * total


def coefficients():
    values = [bessel_scaled(0)]
    for order_index in range(1, ORDER + 1):
        values.append(2.0 * (-1.0) ** order_index * bessel_scaled(order_index))
    return values


def kernel(
    count_hbm, cols_hbm, hub_hbm, send_hbm, row_hbm, embed, tile_val, out,
    sp0, sp1, sp2, sp3, start, tiles, sums, outgoing,
    prev_made, last_made, prev, last, count, cols, hub_ids, send_ids, tile_row, small_sem, table_sem, load_sem, tile_sem, send_sem, recv_sem,
):
    spaces = (sp0, sp1, sp2, sp3)
    coef = coefficients()
    grp = lax.axis_index("grp")
    hub = lax.axis_index("hub")
    x, core = grp // 2, grp % 2
    y, z = hub // 4, hub % 4

    load0 = pltpu.make_async_copy(embed, start, load_sem.at[0])
    load0.start()
    small = [
        pltpu.make_async_copy(there, here, small_sem.at[number])
        for number, (there, here) in enumerate(
            ((hub_hbm, hub_ids), (send_hbm, send_ids), (count_hbm, count), (row_hbm, tile_row), (cols_hbm, cols))
        )
    ]
    for part in small:
        part.start()
    load1 = pltpu.make_async_copy(embed, sp0.at[pl.ds(0, NB)], load_sem.at[1])
    quarter = TILES // 4
    loads = []
    for part in range(4):
        cut = pl.ds(part * quarter, quarter)
        loads.append(pltpu.make_async_copy(tile_val.at[cut], tiles.at[cut], tile_sem.at[part]))

    def place(fam, d1, d2):
        dy, dz = (d2, d1) if fam == 0 else (d1, d2)
        return ((y + dy + 4) % 4) * 4 + (z + dz + 4) % 4

    def tail_group(dx, dc):
        return ((x + dx) % 4) * 2 + (core + dc) % 2

    barrier = pltpu.get_barrier_semaphore()
    friends = [(grp, place(0, d1, d2)) for d1, d2 in ((1, 0), (-1, 0), (2, 0), (0, 1), (0, -1), (0, 2))]
    friends += [(tail_group(dx, dc), hub) for dx, dc in TAILS]
    for friend in friends:
        pl.semaphore_signal(barrier, inc=1, device_id=friend, device_id_type=MESH)

    def hub_copy(step, fam, name, arriving=False):
        (r1, r2), first, count, (t1, t2) = PLAN[name]
        if arriving:
            r1, r2 = r1 - t1, r2 - t2
        r1, r2 = (r1 + 8) % 4, (r2 + 8) % 4
        region = pl.ds(HUB0 + place(fam, r1, r2) * 4 + fam * 2 + first, count)
        ident = fam * NHUB + NAMES.index(name)
        return pltpu.make_async_remote_copy(
            src_ref=spaces[step].at[region],
            dst_ref=spaces[step].at[region],
            send_sem=send_sem.at[ident],
            recv_sem=recv_sem.at[step % 2, ident],
            device_id=(grp, place(fam, t1, t2)),
            device_id_type=MESH,
        )

    def tail_copy(step, number, arriving=False):
        dx, dc = TAILS[number]
        target = tail_group(dx, dc)
        source = tail_group(4 - dx, dc) if arriving else grp
        ident = 2 * NHUB + number
        return pltpu.make_async_remote_copy(
            src_ref=outgoing.at[pl.ds(target * 4, 4)],
            dst_ref=spaces[step].at[pl.ds(TAIL0 + source * 4, 4)],
            send_sem=send_sem.at[ident],
            recv_sem=recv_sem.at[step % 2, ident],
            device_id=(target, hub),
            device_id_type=MESH,
        )

    def row_of(step, row):
        if step == 0:
            return start[row]
        value = sums[last[0, row]] - SHIFT * spaces[step - 1][row].astype(jnp.float32)
        if step >= 2:
            value = 2.0 * value - spaces[step - 2][row].astype(jnp.float32)
        return value.astype(jnp.bfloat16)

    prev_copy = pltpu.make_async_copy(prev_made, prev, table_sem.at[0])
    last_copy = pltpu.make_async_copy(last_made, last, table_sem.at[1])

    def tables():
        across = lax.broadcasted_iota(jnp.int32, (TILES, TILES), 1)
        down = lax.broadcasted_iota(jnp.int32, (TILES, TILES), 0)
        rows = jnp.broadcast_to(tile_row[...], (TILES, TILES))
        live = jnp.where(across < count[0], rows, -1)
        key = jnp.sum(jnp.where(across == down, live, 0), axis=1, keepdims=True)
        before = jnp.max(jnp.where((key == rows) & (down < across), down, -1), axis=0, keepdims=True)
        prev_made[...] = jnp.where(before < 0, TILES, before)
        found = jnp.max(jnp.where(key == across[:, :BLK], down[:, :BLK], -1), axis=0, keepdims=True)
        last_made[...] = jnp.where(found < 0, TILES, found)
        prev_copy.start()
        last_copy.start()

    sums[TILES] = jnp.zeros((BLK, EMB), jnp.float32)
    for part in small:
        part.wait()
    load0.wait()
    pl.semaphore_wait(barrier, len(friends))

    for step in range(ORDER):
        space = spaces[step]

        def go(name):
            for fam in (0, 1):
                hub_copy(step, fam, name).start()

        def pass_on(name, *then):
            for fam in (0, 1):
                hub_copy(step, fam, name, arriving=True).wait_recv()
                for other in then:
                    hub_copy(step, fam, other).start()

        for slot in range(4):
            space[HUB0 + hub * 4 + slot] = row_of(step, hub_ids[0, slot])
        for name in ("m1p", "m1m", "m1d", "s1p0", "s1m0"):
            go(name)
        for number, (dx, dc) in enumerate(TAILS):
            target = tail_group(dx, dc)

            def export(slot, carry):
                outgoing[target * 4 + slot] = row_of(step, send_ids[0, slot, target])
                return carry

            lax.fori_loop(0, 4, export, 0, unroll=True)
            tail_copy(step, number).start()

        def keep_tail(slot, carry):
            space[TAIL0 + grp * 4 + slot] = row_of(step, send_ids[0, slot, grp])
            return carry

        lax.fori_loop(0, 4, keep_tail, 0, unroll=True)

        if step == 0:
            load1.start()
            for part in loads:
                part.start()
            tables()

        def own(pair, carry):
            for inner in range(2):
                row = pair * 2 + inner
                if step == 0:
                    out[row] = coef[0] * start[row].astype(jnp.float32)
                else:
                    value = row_of(step, row)
                    space[row] = value
                    out[row] = out[row] + coef[step] * value.astype(jnp.float32)
            return carry

        lax.fori_loop(0, NB // 4, own, 0)
        pass_on("m1p")
        pass_on("m1m")
        for name in ("s1p-1", "s1m-1", "s1p1", "s1m1"):
            go(name)
        lax.fori_loop(NB // 4, NB // 2, own, 0)
        pass_on("m1d", "s1d2", "s1p2", "s1m2")
        pass_on("s1p0", "s2p0")
        pass_on("s1m0", "s2m0")
        for q in (-1, 1):
            pass_on(f"s1p{q}", f"s2p{q}")
            pass_on(f"s1m{q}", f"s2m{q}")
        for name in ("s1p2", "s1m2", "s1d2", "s2p0", "s2m0", "s2p-1", "s2m-1", "s2p1", "s2m1"):
            pass_on(name)
        for number in range(len(TAILS)):
            tail_copy(step, number, arriving=True).wait_recv()
        for number in range(len(TAILS)):
            tail_copy(step, number).wait_send()
        for fam in (0, 1):
            for name in NAMES:
                hub_copy(step, fam, name).wait_send()
        if step == 0:
            load1.wait()
            for part in loads:
                part.wait()
            prev_copy.wait()
            last_copy.wait()

        def multiply(group, carry):
            for inner in range(UNROLL):
                slot = group * UNROLL + inner
                product = jnp.dot(tiles[slot], space[cols[0, slot]], preferred_element_type=jnp.float32)
                sums[slot] = sums[prev[0, slot]] + product
            return carry

        lax.fori_loop(0, TILES // UNROLL, multiply, 0)

    def finish(pair, carry):
        for inner in range(2):
            row = pair * 2 + inner
            value = row_of(ORDER, row).astype(jnp.float32)
            out[row] = out[row] + coef[ORDER] * value
        return carry

    lax.fori_loop(0, NB // 2, finish, 0)


def shards(embed, hub_ids, send_ids, tile_row, tile_col, tile_val, tile_count):
    hbm = pl.BlockSpec(memory_space=pl.ANY)
    out = pl.pallas_call(
        kernel,
        out_shape=pltpu.VMEM((NB, BLK, EMB), jnp.float32),
        in_specs=[hbm] * 7,
        out_specs=pl.BlockSpec(memory_space=pltpu.VMEM),
        scratch_shapes=[pltpu.VMEM((COLS, BLK, EMB), jnp.bfloat16)] * 4
        + [
            pltpu.VMEM((NB, BLK, EMB), jnp.bfloat16),
            pltpu.VMEM((TILES, BLK, BLK), jnp.bfloat16),
            pltpu.VMEM((TILES + 1, BLK, EMB), jnp.float32),
            pltpu.VMEM((32, BLK, EMB), jnp.bfloat16),
            pltpu.VMEM((1, TILES), jnp.int32),
            pltpu.VMEM((1, BLK), jnp.int32),
            pltpu.SMEM((1, TILES), jnp.int32),
            pltpu.SMEM((1, BLK), jnp.int32),
            pltpu.SMEM((1,), jnp.int32),
            pltpu.SMEM((1, TILES), jnp.int32),
            pltpu.SMEM((1, 4), jnp.int32),
            pltpu.SMEM((1, 4, 8), jnp.int32),
            pltpu.VMEM((1, TILES), jnp.int32),
            pltpu.SemaphoreType.DMA((5,)),
            pltpu.SemaphoreType.DMA((2,)),
            pltpu.SemaphoreType.DMA((2,)),
            pltpu.SemaphoreType.DMA((4,)),
            pltpu.SemaphoreType.DMA((NMSG,)),
            pltpu.SemaphoreType.DMA((2, NMSG)),
        ],
        compiler_params=pltpu.CompilerParams(
            collective_id=0, has_side_effects=True, vmem_limit_bytes=56 * 1024 * 1024
        ),
    )(
        tile_count, tile_col, hub_ids, jnp.swapaxes(send_ids, 1, 2), tile_row,
        embed.reshape(NB, BLK, EMB), tile_val,
    )
    return out.reshape(NB * BLK, EMB)


def solution(mesh):
    both = ("grp", "hub")
    return jax.shard_map(
        shards,
        mesh=mesh,
        in_specs=(
            P(both, None), P(both, None), P(both, None, None), P(both, None),
            P(both, None), P(both, None, None), P(both),
        ),
        out_specs=P(both, None),
        check_vma=False,
    )
```

time: 107 us -> 82.3 us (0.77); the launches traced: 106 us -> 82.1 us
  Pallas kernels: 96.4 us -> 79.5 us
  local copies, waits for them, and re-layouts: 5.85 us -> 2.02 us
  other arithmetic: 2.76 us -> 0 us
    pallas_call x1, Pallas kernels: 96.4 us -> 79.5 us  [shards(): pl.pallas_call(kernel, out_shape=pltpu.VMEM((NB, BLK, EMB), jnp.float32),...]
    unnamed x2 -> x1, local copies, waits for them, and re-layouts: 5.23 us -> 2.02 us
    select_n x3 -> x0, other arithmetic: 1.77 us -> none  [the longest x1 0.69 us: shards(): key = jnp.where(slots < tile_count[0], rows, -1)]
where the time goes in v2:
time: 82.3 us; the launch traced here: 82.1 us
  Pallas kernels  79.5 us (97%)
  local copies, waits for them, and re-layouts  2.02 us (2%)
    pallas_call x1, Pallas kernels, shards(): pl.pallas_call(kernel, out_shape=pltpu.VMEM((NB, BLK, EMB), jnp.float32),...  79.5 us
    unnamed x1, local copies, waits for them, and re-layouts  2.02 us

profile of v2, /device:TPU:4, one launch (start us, length us, event | category | flops | bytes accessed | tf_op | source)
XLA Modules:
  0.0 82.1 jit_solution(14379735859721563642)
XLA Ops:
  0.7 79.5 %shard_map.73 = f32[64,128,128]{2,1,0:T(8,128)S(1)} custom-call(s32[1]{0:T(128)S(6)} %copy.10.count_hbm, s32[1,192]{1,0:T(1,128)} %cols_hbm.1, s32[1,4]{1,0:T(1,128)} %hub_hbm.1, s32[1,4,8]{2,1,0:T(4,128)} %bitcast.5, s32[1,192]{1,0:T(1,128)} %row_hbm.1, bf16[64,128,128]{2,1,0:T(8,128)(2,1)} %bitcast.4, bf16[192,128,128]{2,1,0:T(8,128)(2,1)} %tile_val.1), custom_call_target="tpu_custom_call" | custom-call | tf_op jit(solution)/shard_map/pallas_call | solution.py:261
  80.1 2.0 %copy.9 = f32[8192,128]{1,0:T(8,128)} copy(f32[8192,128]{1,0:T(8,128)S(1)} %bitcast.3) | data formatting | bytes 8388608

commit v3 on v2

--- a/solution.py
+++ b/solution.py
@@ -20,7 +20,7 @@
 COLS = 160
 BLK = 128
 EMB = 128
-UNROLL = 48
+UNROLL = 96
 
 TAILS = ((2, 0), (2, 1), (1, 0), (1, 1), (3, 0), (3, 1), (0, 1))
 PLAN = {

time: 82.3 us -> 81.3 us (0.988)
  Pallas kernels: 79.5 us -> 78.5 us
    pallas_call x1, Pallas kernels: 79.5 us -> 78.5 us  [shards(): pl.pallas_call(kernel, out_shape=pltpu.VMEM((NB, BLK, EMB), jnp.float32),...]
where the time goes in v3:
time: 81.3 us; the launch traced here: 81.2 us
  Pallas kernels  78.5 us (97%)
  local copies, waits for them, and re-layouts  2.02 us (2%)
    pallas_call x1, Pallas kernels, shards(): pl.pallas_call(kernel, out_shape=pltpu.VMEM((NB, BLK, EMB), jnp.float32),...  78.5 us
    unnamed x1, local copies, waits for them, and re-layouts  2.02 us

profile of v3, /device:TPU:4, one launch (start us, length us, event | category | flops | bytes accessed | tf_op | source)
XLA Modules:
  0.0 81.2 jit_solution(10688098063232111052)
XLA Ops:
  0.7 78.5 %shard_map.73 = f32[64,128,128]{2,1,0:T(8,128)S(1)} custom-call(s32[1]{0:T(128)S(6)} %copy.10.count_hbm, s32[1,192]{1,0:T(1,128)} %cols_hbm.1, s32[1,4]{1,0:T(1,128)} %hub_hbm.1, s32[1,4,8]{2,1,0:T(4,128)} %bitcast.5, s32[1,192]{1,0:T(1,128)} %row_hbm.1, bf16[64,128,128]{2,1,0:T(8,128)(2,1)} %bitcast.4, bf16[192,128,128]{2,1,0:T(8,128)(2,1)} %tile_val.1), custom_call_target="tpu_custom_call" | custom-call | tf_op jit(solution)/shard_map/pallas_call | solution.py:261
  79.2 2.0 %copy.9 = f32[8192,128]{1,0:T(8,128)} copy(f32[8192,128]{1,0:T(8,128)S(1)} %bitcast.3) | data formatting | bytes 8388608
